TPU v7x, 32 devices: a whole 2x2x4 slice. The times are simulated.
32 devices in a mesh: pair: 4 (over x, core), row: 2 (over y), col: 4 (over z).
Axes of the slice: x: 2, y: 2, z: 4, core: 2. Of those that a mesh axis runs over, the one named last changes fastest.
Arguments:
- coords: float32 [4, 30, 512], P('pair', None, ('row', 'col')), may hold values from -1.6 to 1.6
- final_coords: float32 [30, 512], P(None, ('row', 'col')), may hold values from -1.6 to 1.6
- growth: float32 [4, 512], P('pair', ('row', 'col')), may hold values from 0.4 to 2.5
- counts: int32 [5], replicated, may hold values from 256 to 512, as said below
- labels: int32 [512], P(('row', 'col')), may hold values from 0 to 15
Outputs:
- fates: float32 [4, 16, 512], P('pair', None, ('row', 'col'))
- mass: float32 [4, 512], P('pair', ('row', 'col'))
Inputs may be any that keep to these rules, and one draw needn't show every extreme that they name: The cells of a timepoint are its first counts positions; some timepoint has all 512.
All inputs are finite; a program needn't handle non-finite values.
Results may differ from a plain program's by a relative error of at most 0.0001.
Values sent between devices are 32-bit elements; how exact they have to be, the bound alone decides.
A program may use at most 64 MiB of HBM per device.

v0:
```python
import jax
import jax.numpy as jnp
from jax import lax
from jax.sharding import PartitionSpec as P

CLASSES = 16


cost_scale = 1.0
source_power = 0.5
target_power = 50.0 / 51.0


def shifted_2(block, axis, distance):
    devices = range(lax.axis_size(axis))
    route = [(i - distance, i) for i in devices if i - distance in devices]
    return lax.ppermute(block, axis, route)


def kernel_tile(sources, targets):
    cross = lax.dot_general(
        sources,
        targets,
        (((0,), (0,)), ((), ())),
        precision=lax.Precision.HIGHEST,
        preferred_element_type=jnp.float32,
    )
    source_norms = jnp.sum(sources * sources, axis=0)
    target_norms = jnp.sum(targets * targets, axis=0)
    return jnp.exp(-(source_norms[:, None] + target_norms[None, :] - 2.0 * cross) / cost_scale)


def forward(kernel, weights):
    return lax.dot_general(
        weights,
        kernel,
        (((1,), (1,)), ((), ())),
        precision=lax.Precision.HIGHEST,
        preferred_element_type=jnp.float32,
    )


def backward(kernel, scales):
    return jnp.dot(
        scales, kernel, precision=lax.Precision.HIGHEST, preferred_element_type=jnp.float32
    )


def per_device(coords, final_coords, growth, counts, labels):
    tile = coords.shape[2]
    n_pair = lax.axis_size("pair")
    n_row = lax.axis_size("row")
    n_col = lax.axis_size("col")
    pair_at = lax.axis_index("pair")
    row_at = lax.axis_index("row")
    col_at = lax.axis_index("col")
    source_count = n_col * tile
    target_count = n_row * tile
    own_coords = coords[0]
    sources, source_growth = (
        lax.all_gather(own_coords, "col", axis=1, tiled=True),
        lax.all_gather(growth[0], "col", axis=0, tiled=True),
    )
    shifted = shifted_2(own_coords, "pair", -1)
    is_last = pair_at == n_pair - 1
    own_targets = jnp.where(is_last, final_coords, shifted)
    label_values = labels.astype(jnp.float32)
    position = lax.iota(jnp.int32, target_count)
    targets, target_labels = (
        lax.all_gather(own_targets, "row", axis=1, tiled=True),
        lax.all_gather(label_values, "row", axis=0, tiled=True),
    )
    target_index = position // tile * (n_col * tile) + col_at * tile + position % tile

    def hand_over(fates_now):
        incoming = shifted_2(fates_now, "pair", -1)
        return lax.all_gather(incoming, "row", axis=1, tiled=True)

    source_number = counts[pair_at]
    target_number = counts[pair_at + 1]
    source_total = source_number.astype(jnp.float32)
    target_total = target_number.astype(jnp.float32)
    source_index = row_at * source_count + lax.iota(jnp.int32, source_count)
    source_valid = source_index < source_number
    target_valid = target_index < target_number
    kernel = kernel_tile(sources, targets)
    start_terms = forward(kernel, target_valid.astype(jnp.float32)[None, :])[0]
    start_rows = lax.psum(start_terms, "col")
    source_mass = jnp.where(source_valid, source_growth / source_total, 0.0)
    scale_u = jnp.where(source_valid, jnp.power(source_mass / start_rows, source_power), 0.0)
    column_terms = backward(kernel, scale_u)
    column_totals = lax.psum(column_terms, "row")
    target_mass = target_valid.astype(jnp.float32) / target_total
    scale_v = jnp.where(target_valid, jnp.power(target_mass / column_totals, target_power), 0.0)
    own_offset = col_at * tile
    own_valid = lax.dynamic_slice_in_dim(source_valid, own_offset, tile, 0)
    own_scale = lax.dynamic_slice_in_dim(scale_u, own_offset, tile, 0)
    class_values = lax.iota(jnp.int32, CLASSES).astype(jnp.float32)
    label_table = jnp.where(
        (target_labels[None, :] == class_values[:, None]) & target_valid[None, :], 1.0, 0.0
    ).astype(jnp.float32)
    empty = jnp.zeros((CLASSES, tile), jnp.float32)
    final_terms = forward(kernel, scale_v[None, :])[0]
    final_rows = lax.psum(final_terms, "col")
    own_rows = lax.dynamic_slice_in_dim(final_rows, own_offset, tile, 0)
    safe_rows = jnp.where(own_valid, own_rows, 1.0)

    def advance(turn, fates_now):
        carried = jnp.where(is_last, label_table, hand_over(fates_now))
        terms = forward(kernel, carried * scale_v[None, :])
        sums = lax.psum_scatter(terms, "col", scatter_dimension=1, tiled=True)
        return jnp.where(own_valid[None, :], sums / safe_rows[None, :], 0.0)

    fates = lax.fori_loop(0, n_pair, advance, empty)
    mass = jnp.where(own_valid, source_total * own_scale * own_rows, 0.0)
    return (fates[None], mass[None])


def solution(mesh):
    placed = (
        P("pair", None, ("row", "col")),
        P(None, ("row", "col")),
        P("pair", ("row", "col")),
        P(),
        P(("row", "col")),
    )
    return jax.shard_map(
        per_device,
        mesh=mesh,
        in_specs=placed,
        out_specs=(P("pair", None, ("row", "col")), P("pair", ("row", "col"))),
        check_vma=False,
    )
```

profile of v0, /device:TPU:0, one launch (start us, length us, event | category | flops | bytes accessed | tf_op | source)
XLA Modules:
  0.0 184.0 jit_solution(5773069660828928594)
XLA Ops:
  7.2 0.8 copy.19
  8.0 1.3 collective-permute-start.1
  9.4 0.7 copy-done.7
  10.0 0.6 dynamic-slice.1
  10.7 0.6 dynamic-slice
  12.6 15.2 %all-gather.1 = f32[1,30,256]{1,0,2:T(1,128)S(1)} all-gather(f32[1,30,64]{1,0,2:T(1,128)S(1)} %copy.12), channel_id=3, replica_groups=mesh['pair'=4,'row'=2,'col'=4] {'col'}, dimensions={2}, use_global_device_ids=true | all-gather | bytes 38400 | tf_op jit(solution)/shard_map/all_gather | solution.py:61
  27.9 0.6 copy-done.3
  28.6 0.6 fusion.29
  29.2 0.7 copy-done.4
  29.9 0.7 copy-done.5
  30.7 0.7 fusion.24
  32.7 4.4 %all-gather.3 = f32[2,64,30]{1,2,0:T(8,128)S(1)} all-gather(f32[1,64,30]{1,2,0:T(8,128)S(1)} %select_bitcast_fusion), channel_id=1, replica_groups=mesh['pair'=4,'row'=2,'col'=4] {'row'}, dimensions={0}, use_global_device_ids=true | all-gather | bytes 23040 | tf_op jit(solution)/shard_map/all_gather | solution.py:70
  37.3 0.3 fusion.19
  37.7 0.2 fusion.20
  37.8 11.8 %all-reduce.2 = (f32[256]{0:T(256)S(1)}, f32[256]{0:T(256)S(1)}) all-reduce(f32[256]{0:T(256)S(1)} %bitcast.75, f32[256]{0:T(256)S(1)} %bitcast_dynamic-update-slice_fusion), channel_id=1, replica_groups=mesh['pair'=4,'row'=2,'col'=4] {'col'}, use_global_device_ids=true, to_apply=%region_2.3 | all-reduce | flops 512 | bytes 4096 | tf_op jit(solution)/shard_map/psum | solution.py:88
  49.7 0.7 power_select_fusion
  50.3 0.2 convolution_bitcast_fusion.1
  50.5 5.0 %all-reduce.3 = (f32[128]{0:T(128)S(1)}, f32[128]{0:T(128)S(1)}) all-reduce(f32[128]{0:T(128)S(1)} %convolution_bitcast_fusion.1, f32[128]{0:T(128)S(1)} %convert_dynamic-update-slice_fusion), channel_id=1, replica_groups=mesh['pair'=4,'row'=2,'col'=4] {'row'}, use_global_device_ids=true, to_apply=%region_3.4 | all-reduce | flops 256 | bytes 2048 | tf_op jit(solution)/shard_map/psum | solution.py:92
  55.5 0.6 power_select_fusion.1
  56.1 0.2 fusion.27
  56.3 8.4 %psum.23 = f32[256]{0:T(256)S(1)} all-reduce(f32[256]{0:T(256)S(1)} %bitcast.76), channel_id=1, replica_groups=mesh['pair'=4,'row'=2,'col'=4] {'col'}, use_global_device_ids=true, to_apply=%region_4.5 | all-reduce | flops 256 | bytes 2048 | tf_op jit(solution)/shard_map/psum | solution.py:104
  64.6 0.6 select_bitcast_fusion.1
  65.3 111.6 %while.11 = (s32[]{:T(128)}, f32[16,64]{1,0:T(8,128)S(1)}, pred[64]{0:T(512)(128)(4,1)S(1)}, pred[]{:T(512)}, f32[128]{0:T(128)S(1)}, /*index=5*/f32[256,128]{1,...) while((s32[]{:T(128)}, f32[16,64]{1,0:T(8,128)S(1)}, ...), condition=%wide.region_7.8_spmd.clone, body=%wide.region_5.7_spmd.clone.sunk | while | flops 6304771 | bytes 448208 | solution.py:114
  65.3 1.3 collective-permute-start
  66.6 1.8 collective-permute-done
  68.4 4.3 %all-gather.6 = f32[2,64,16]{1,2,0:T(8,128)S(1)} all-gather(f32[1,64,16]{1,2,0:T(8,128)S(1)} %bitcast.71), channel_id=1, replica_groups=mesh['pair'=4,'row'=2,'col'=4] {'row'}, dimensions={0}, use_global_device_ids=true | all-gather | bytes 12288 | tf_op jit(solution)/shard_map/while/body/eval_jaxpr/all_gather | solution.py:77
  72.8 1.0 convolution_bitcast_fusion.3
  73.8 20.1 %reduce-scatter.6.cloned.1.call-done = f32[64,16]{1,0:T(8,128)} async-done(((f32[256,16]{1,0:T(8,128)}), f32[64,16]{1,0:T(8,128)}) %reduce-scatter.6.cloned.1.call-update) | async-done | bytes 4112 | tf_op jit(solution)/shard_map/while
  93.9 0.8 copy.23
  94.8 1.3 collective-permute-start
  96.1 1.8 collective-permute-done
  97.8 4.3 %all-gather.6 = f32[2,64,16]{1,2,0:T(8,128)S(1)} all-gather(f32[1,64,16]{1,2,0:T(8,128)S(1)} %bitcast.71), channel_id=1, replica_groups=mesh['pair'=4,'row'=2,'col'=4] {'row'}, dimensions={0}, use_global_device_ids=true | all-gather | bytes 12288 | tf_op jit(solution)/shard_map/while/body/eval_jaxpr/all_gather | solution.py:77
  102.3 1.0 convolution_bitcast_fusion.3
  103.3 17.9 %reduce-scatter.6.cloned.1.call-done = f32[64,16]{1,0:T(8,128)} async-done(((f32[256,16]{1,0:T(8,128)}), f32[64,16]{1,0:T(8,128)}) %reduce-scatter.6.cloned.1.call-update) | async-done | bytes 4112 | tf_op jit(solution)/shard_map/while
  121.2 0.8 copy.23
  122.1 1.3 collective-permute-start
  123.4 1.8 collective-permute-done
  125.2 4.3 %all-gather.6 = f32[2,64,16]{1,2,0:T(8,128)S(1)} all-gather(f32[1,64,16]{1,2,0:T(8,128)S(1)} %bitcast.71), channel_id=1, replica_groups=mesh['pair'=4,'row'=2,'col'=4] {'row'}, dimensions={0}, use_global_device_ids=true | all-gather | bytes 12288 | tf_op jit(solution)/shard_map/while/body/eval_jaxpr/all_gather | solution.py:77
  129.6 1.0 convolution_bitcast_fusion.3
  130.6 18.1 %reduce-scatter.6.cloned.1.call-done = f32[64,16]{1,0:T(8,128)} async-done(((f32[256,16]{1,0:T(8,128)}), f32[64,16]{1,0:T(8,128)}) %reduce-scatter.6.cloned.1.call-update) | async-done | bytes 4112 | tf_op jit(solution)/shard_map/while
  148.7 0.8 copy.23
  149.6 1.3 collective-permute-start
  150.9 1.8 collective-permute-done
  152.6 4.3 %all-gather.6 = f32[2,64,16]{1,2,0:T(8,128)S(1)} all-gather(f32[1,64,16]{1,2,0:T(8,128)S(1)} %bitcast.71), channel_id=1, replica_groups=mesh['pair'=4,'row'=2,'col'=4] {'row'}, dimensions={0}, use_global_device_ids=true | all-gather | bytes 12288 | tf_op jit(solution)/shard_map/while/body/eval_jaxpr/all_gather | solution.py:77
  157.1 1.0 convolution_bitcast_fusion.3
  158.1 17.9 %reduce-scatter.6.cloned.1.call-done = f32[64,16]{1,0:T(8,128)} async-done(((f32[256,16]{1,0:T(8,128)}), f32[64,16]{1,0:T(8,128)}) %reduce-scatter.6.cloned.1.call-update) | async-done | bytes 4112 | tf_op jit(solution)/shard_map/while
  176.0 0.8 copy.23
  176.9 0.6 copy-done
  (50 shorter events, 1.3 us)
Async XLA Ops:
  7.2 2.1 %copy-start.1 = (f32[1,30,64]{2,0,1:T(1,128)S(1)}, f32[1,30,64]{2,0,1:T(1,128)}, u32[]{:S(2)}) copy-start(f32[1,30,64]{2,0,1:T(1,128)} %param.7) | copy-start | bytes 23044
  8.0 24.7 %collective-permute-start.1 = (f32[30,64]{1,0:T(8,128)S(1)}, f32[30,64]{1,0:T(8,128)S(1)}, u32[]{:S(2)}, u32[]{:S(2)}) collective-permute-start(f32[30,64]{1,0:T(8,128)S(1)} %bitcast.73), channel_id=1, source_target_pairs={{8,0},{16,8},{24,16},{9,1},{17,9},{25,17},{10,2},{18,10},{26,18},{... | collective-permute-start | bytes 23048 | tf_op jit(solution)/shard_map/ppermute | solution.py:17
  9.4 0.7 copy-start.7
  10.0 0.7 copy-start.6
  27.9 0.7 copy-start.3
  29.2 0.7 copy-start.4
  29.9 0.7 copy-start.5
  30.7 2.0 %copy-start.2 = (f32[30,64]{1,0:T(8,128)S(1)}, f32[30,64]{1,0:T(8,128)}, u32[]{:S(2)}) copy-start(f32[30,64]{1,0:T(8,128)} %param.8) | copy-start | bytes 23044
  65.3 28.6 %reduce-scatter.6.cloned.1.call-start = ((), (), s32[]{:S(2)}) async-start(), calls=%async_computation.1 | async-start | bytes 163840 | tf_op jit(solution)/shard_map/while
  65.3 3.1 %collective-permute-start = (f32[16,64]{1,0:T(8,128)S(1)}, f32[16,64]{1,0:T(8,128)S(1)}, u32[]{:S(2)}, u32[]{:S(2)}) collective-permute-start(f32[16,64]{1,0:T(8,128)S(1)} %broadcast_select_fusion.3), channel_id=1, source_target_pairs={{8,0},{16,8},{24,16},{9,1},{17,9},{25,17},{10,2},{18,10},{26,18},{... | collective-permute-start | bytes 12296 | tf_op jit(solution)/shard_map/while/body/eval_jaxpr/ppermute | solution.py:17
  94.7 26.5 %reduce-scatter.6.cloned.1.call-start = ((), (), s32[]{:S(2)}) async-start(), calls=%async_computation.1 | async-start | bytes 163840 | tf_op jit(solution)/shard_map/while
  94.8 3.1 %collective-permute-start = (f32[16,64]{1,0:T(8,128)S(1)}, f32[16,64]{1,0:T(8,128)S(1)}, u32[]{:S(2)}, u32[]{:S(2)}) collective-permute-start(f32[16,64]{1,0:T(8,128)S(1)} %broadcast_select_fusion.3), channel_id=1, source_target_pairs={{8,0},{16,8},{24,16},{9,1},{17,9},{25,17},{10,2},{18,10},{26,18},{... | collective-permute-start | bytes 12296 | tf_op jit(solution)/shard_map/while/body/eval_jaxpr/ppermute | solution.py:17
  122.0 26.6 %reduce-scatter.6.cloned.1.call-start = ((), (), s32[]{:S(2)}) async-start(), calls=%async_computation.1 | async-start | bytes 163840 | tf_op jit(solution)/shard_map/while
  122.1 3.1 %collective-permute-start = (f32[16,64]{1,0:T(8,128)S(1)}, f32[16,64]{1,0:T(8,128)S(1)}, u32[]{:S(2)}, u32[]{:S(2)}) collective-permute-start(f32[16,64]{1,0:T(8,128)S(1)} %broadcast_select_fusion.3), channel_id=1, source_target_pairs={{8,0},{16,8},{24,16},{9,1},{17,9},{25,17},{10,2},{18,10},{26,18},{... | collective-permute-start | bytes 12296 | tf_op jit(solution)/shard_map/while/body/eval_jaxpr/ppermute | solution.py:17
  149.5 26.5 %reduce-scatter.6.cloned.1.call-start = ((), (), s32[]{:S(2)}) async-start(), calls=%async_computation.1 | async-start | bytes 163840 | tf_op jit(solution)/shard_map/while
  149.6 3.1 %collective-permute-start = (f32[16,64]{1,0:T(8,128)S(1)}, f32[16,64]{1,0:T(8,128)S(1)}, u32[]{:S(2)}, u32[]{:S(2)}) collective-permute-start(f32[16,64]{1,0:T(8,128)S(1)} %broadcast_select_fusion.3), channel_id=1, source_target_pairs={{8,0},{16,8},{24,16},{9,1},{17,9},{25,17},{10,2},{18,10},{26,18},{... | collective-permute-start | bytes 12296 | tf_op jit(solution)/shard_map/while/body/eval_jaxpr/ppermute | solution.py:17
  176.9 0.6 copy-start
Sparse Core Ops, SparseCore 0:
  73.9 19.9 reduce-scatter.5
  103.4 17.7 reduce-scatter.5
  130.7 17.9 reduce-scatter.5
  158.2 17.7 reduce-scatter.5
where the time goes:
time: 185 us; the launch traced here: 184 us
  waiting for transfers between devices  81.2 us (44%)
  blocking collectives  62.1 us (34%)
  between operations  16.5 us (9%)
  local copies, waits for them, and re-layouts  9.93 us (5%)
  starting transfers between devices  6.55 us (4%)
  matrix products  4.65 us (3%)
  other arithmetic  2.9 us (2%)
    while x8, waiting for transfers between devices  74.1 us
    all_gather x4, blocking collectives, hand_over(): return lax.all_gather(incoming, 'row', axis=1, tiled=True)  17.4 us
    all_gather x1, blocking collectives, per_device(): lax.all_gather(own_coords, 'col', axis=1, tiled=True)  15.2 us
    psum x1, blocking collectives, per_device(): start_rows = lax.psum(start_terms, 'col')  11.8 us
    psum x1, blocking collectives, per_device(): final_rows = lax.psum(final_terms, 'col')  8.37 us
    ppermute x5, waiting for transfers between devices, shifted_2(): return lax.ppermute(block, axis, route)  7.07 us
    ppermute x5, starting transfers between devices, shifted_2(): return lax.ppermute(block, axis, route)  6.45 us
    unnamed x25, local copies, waits for them, and re-layouts  5.66 us
  transfers between devices with their start and end apart: 9, of which 8 were waited for; matrix products, arithmetic and copies ran while one was open for 2% of the time, Pallas kernels for 0%

commit v1 on v0

--- a/solution.py
+++ b/solution.py
@@ -1,9 +1,13 @@
+import functools
 import jax
 import jax.numpy as jnp
 from jax import lax
+from jax.experimental import pallas as pl
+from jax.experimental.pallas import tpu as pltpu
 from jax.sharding import PartitionSpec as P
 
 CLASSES = 16
+FUSED_BYTES = 16 * 1024 * 1024
 
 
 cost_scale = 1.0
@@ -116,6 +120,326 @@
     return (fates[None], mass[None])
 
 
+LANES = 128
+HALF = 16
+BIG = 1e30
+MESH = pl.DeviceIdType.MESH
+
+
+def split3(a):
+    first = a.astype(jnp.bfloat16)
+    rest = a - first.astype(jnp.float32)
+    second = rest.astype(jnp.bfloat16)
+    third = (rest - second.astype(jnp.float32)).astype(jnp.bfloat16)
+    return first, second, third
+
+
+def split2(a):
+    first = a.astype(jnp.bfloat16)
+    return first, (a - first.astype(jnp.float32)).astype(jnp.bfloat16)
+
+
+def dot(a, b, dims):
+    return lax.dot_general(a, b, (dims, ((), ())), preferred_element_type=jnp.float32)
+
+
+def packed(block, extra):
+    low = block[:HALF]
+    rest = block.shape[0] - HALF
+    fill = jnp.zeros((HALF - rest - 1, block.shape[1]), jnp.float32)
+    high = jnp.concatenate([block[HALF:], extra, fill], axis=0)
+    return jnp.concatenate([low, high], axis=1)
+
+
+def unpacked(ref):
+    lows, highs = [], []
+    lane = lax.broadcasted_iota(jnp.int32, (HALF, LANES), 1)
+    for j in range(ref.shape[0] // 2):
+        a, b = ref[2 * j], ref[2 * j + 1]
+        swap_a, swap_b = pltpu.roll(a, LANES // 2, 1), pltpu.roll(b, LANES // 2, 1)
+        lows.append(jnp.where(lane < LANES // 2, a, swap_b))
+        highs.append(jnp.where(lane < LANES // 2, swap_a, b))
+    low, high = jnp.concatenate(lows, axis=1), jnp.concatenate(highs, axis=1)
+    return jnp.concatenate([low, high], axis=0)
+
+
+def own_part(ref, value, mine, tile):
+    for j in range(ref.shape[0]):
+        ref[j] = value[:, j * LANES : (j + 1) * LANES]
+    chunk = ref[mine // 2]
+    return pltpu.roll(chunk, (mine % 2) * tile, 1)[:, :tile]
+
+
+def fused(
+    sizes,
+    counts_ref,
+    coords_ref,
+    final_ref,
+    growth_ref,
+    labels_ref,
+    fates_ref,
+    mass_ref,
+    xg,
+    yg,
+    k1,
+    k2,
+    fin,
+    fout,
+    pick_f,
+    pick_m,
+    x_send,
+    x_recv,
+    y_send,
+    y_recv,
+    f_send,
+    f_recv,
+):
+    n_pair, n_row, n_col, tile = sizes
+    n_block = n_row * n_col
+    cells = n_block * tile
+    pca = coords_ref.shape[1]
+    last = n_pair - 1
+    pair_at = lax.axis_index("pair")
+    row_at = lax.axis_index("row")
+    col_at = lax.axis_index("col")
+    mine = row_at * n_col + col_at
+    is_last = pair_at == last
+    not_last = pair_at < last
+    not_first = pair_at > 0
+
+    def peer(step):
+        other = lax.rem(mine + step, n_block)
+        return other, other // n_col, lax.rem(other, n_col)
+
+    barrier = pltpu.get_barrier_semaphore()
+    for step in range(1, n_block):
+        _, r, c = peer(step)
+        pl.semaphore_signal(barrier, inc=1, device_id=(pair_at, r, c), device_id_type=MESH)
+
+    @pl.when(not_last)
+    def _():
+        for step in range(n_block):
+            _, r, c = peer(step)
+            pl.semaphore_signal(
+                barrier, inc=1, device_id=(pair_at + 1, r, c), device_id_type=MESH
+            )
+
+    xg[mine] = packed(coords_ref[0], growth_ref[...])
+
+    @pl.when(is_last)
+    def _():
+        yg[mine] = packed(final_ref[...], labels_ref[...].astype(jnp.float32))
+
+    @pl.when(not_first)
+    def _():
+        pl.semaphore_wait(barrier, 2 * n_block - 1)
+
+    @pl.when(pair_at == 0)
+    def _():
+        pl.semaphore_wait(barrier, n_block - 1)
+
+    def x_copy(step):
+        other, r, c = peer(step)
+        return pltpu.make_async_remote_copy(
+            src_ref=xg.at[mine],
+            dst_ref=xg.at[mine],
+            send_sem=x_send.at[step],
+            recv_sem=x_recv.at[mine],
+            device_id=(pair_at, r, c),
+            device_id_type=MESH,
+        )
+
+    def y_copy(step, source, pair):
+        other, r, c = peer(step)
+        return pltpu.make_async_remote_copy(
+            src_ref=source.at[mine],
+            dst_ref=yg.at[mine],
+            send_sem=y_send.at[step],
+            recv_sem=y_recv.at[mine],
+            device_id=(pair, r, c),
+            device_id_type=MESH,
+        )
+
+    def arrival(buffer, sems, other):
+        return pltpu.make_async_remote_copy(
+            src_ref=buffer.at[other],
+            dst_ref=buffer.at[other],
+            send_sem=x_send.at[0],
+            recv_sem=sems.at[other],
+            device_id=(pair_at, row_at, col_at),
+            device_id_type=MESH,
+        )
+
+    for step in range(1, n_block):
+        x_copy(step).start()
+
+    @pl.when(not_first)
+    def _():
+        for step in range(n_block):
+            y_copy(step, xg, pair_at - 1).start()
+
+    z_send = f_send
+
+    @pl.when(is_last)
+    def _():
+        for step in range(1, n_block):
+            other, r, c = peer(step)
+            pltpu.make_async_remote_copy(
+                src_ref=yg.at[mine],
+                dst_ref=yg.at[mine],
+                send_sem=z_send.at[step],
+                recv_sem=y_recv.at[mine],
+                device_id=(pair_at, r, c),
+                device_id_type=MESH,
+            ).start()
+
+    for step in range(1, n_block):
+        other, _, _ = peer(step)
+        arrival(xg, x_recv, other).wait_recv()
+    for step in range(1, n_block):
+        other, _, _ = peer(step)
+        arrival(yg, y_recv, other).wait_recv()
+
+    @pl.when(not_last)
+    def _():
+        arrival(yg, y_recv, mine).wait_recv()
+
+    source_number = counts_ref[pair_at]
+    target_number = counts_ref[pair_at + 1]
+    source_total = source_number.astype(jnp.float32)
+    target_total = target_number.astype(jnp.float32)
+    index = lax.broadcasted_iota(jnp.int32, (1, cells), 1)
+    source_valid = index < source_number
+    target_valid = index < target_number
+
+    x = unpacked(xg)
+    y = unpacked(yg)
+    growth = x[pca : pca + 1]
+    labels = y[pca : pca + 1]
+    feature = lax.broadcasted_iota(jnp.int32, x.shape, 0)
+    x = jnp.where(feature < pca, x, 0.0)
+    y = jnp.where(feature < pca, y, 0.0)
+    x_norm = jnp.sum(x * x, axis=0, keepdims=True)
+    y_norm = jnp.where(target_valid, jnp.sum(y * y, axis=0, keepdims=True), BIG)
+    a = jnp.where(feature < pca, x + x, jnp.where(feature == pca, -x_norm, 1.0))
+    b = jnp.where(feature < pca, y, jnp.where(feature == pca, 1.0, -y_norm))
+    a1, a2, a3 = split3(a)
+    b1, b2, b3 = split3(b)
+    left = jnp.concatenate([b1, b1, b2, b2, b1, b3], axis=0)
+    right = jnp.concatenate([a1, a2, a1, a2, a3, a1], axis=0)
+    totals = jnp.zeros((1, cells), jnp.float32)
+    for j in range(cells // LANES):
+        rows = slice(j * LANES, (j + 1) * LANES)
+        values = jnp.exp(dot(left[:, rows], right, ((0,), (0,))))
+        totals = totals + jnp.sum(values, axis=0, keepdims=True)
+        high, low = split2(values)
+        k1[rows, :] = high
+        k2[rows, :] = low
+    scale_u = jnp.where(source_valid, jnp.sqrt(growth / source_total / totals), 0.0)
+    u1, u2 = split2(jnp.broadcast_to(scale_u, (HALF, cells)))
+    u12 = jnp.concatenate([u1, u2], axis=0)
+    column = dot(u12, k1[...], ((1,), (1,)))
+    column_low = dot(u1, k2[...], ((1,), (1,)))
+    column = column[:1] + column[HALF : HALF + 1] + column_low[:1]
+    ratio = 1.0 / target_total / jnp.where(target_valid, column, 1.0)
+    scale_v = jnp.where(target_valid, jnp.exp(target_power * jnp.log(ratio)), 0.0)
+
+    def transported(weights):
+        w1, w2 = split2(weights)
+        both = dot(jnp.concatenate([w1, w2], axis=0), k1[...], ((1,), (0,)))
+        return both[:CLASSES] + both[CLASSES:] + dot(w1, k2[...], ((1,), (0,)))
+
+    row_totals = transported(jnp.broadcast_to(scale_v, (CLASSES, cells)))[:1]
+    mass = jnp.where(source_valid, source_total * scale_u * row_totals, 0.0)
+    mass_ref[...] = own_part(pick_m, jnp.broadcast_to(mass, (8, cells)), mine, tile)[:1]
+    share = jnp.where(source_valid, 1.0 / row_totals, 0.0)
+
+    f_copy = pltpu.make_async_remote_copy(
+        src_ref=fout,
+        dst_ref=fin,
+        send_sem=f_send.at[0],
+        recv_sem=f_recv,
+        device_id=(jnp.maximum(pair_at - 1, 0), row_at, col_at),
+        device_id_type=MESH,
+    )
+
+    @pl.when(is_last)
+    def _():
+        class_values = lax.broadcasted_iota(jnp.int32, (CLASSES, cells), 0).astype(jnp.float32)
+        fin[...] = jnp.where((labels == class_values) & target_valid, 1.0, 0.0)
+
+    @pl.when(not_last)
+    def _():
+        f_copy.wait_recv()
+
+    fates = transported(fin[...] * scale_v) * share
+    fout[...] = fates
+
+    @pl.when(not_first)
+    def _():
+        f_copy.start()
+
+    fates_ref[0] = own_part(pick_f, fates, mine, tile)
+
+    for step in range(1, n_block):
+        x_copy(step).wait_send()
+
+    @pl.when(not_first)
+    def _():
+        for step in range(n_block):
+            y_copy(step, xg, pair_at - 1).wait_send()
+        f_copy.wait_send()
+
+    @pl.when(is_last)
+    def _():
+        for step in range(1, n_block):
+            pltpu.make_async_remote_copy(
+                src_ref=yg.at[mine],
+                dst_ref=yg.at[mine],
+                send_sem=z_send.at[step],
+                recv_sem=y_recv.at[mine],
+                device_id=(pair_at, row_at, col_at),
+                device_id_type=MESH,
+            ).wait_send()
+
+
+def per_device_fused(coords, final_coords, growth, counts, labels):
+    tile = coords.shape[2]
+    n_pair = lax.axis_size("pair")
+    n_row = lax.axis_size("row")
+    n_col = lax.axis_size("col")
+    n_block = n_row * n_col
+    cells = n_block * tile
+    vmem = pl.BlockSpec(memory_space=pltpu.VMEM)
+    dma = pltpu.SemaphoreType.DMA
+    return pl.pallas_call(
+        functools.partial(fused, (n_pair, n_row, n_col, tile)),
+        out_shape=(
+            jax.ShapeDtypeStruct((1, CLASSES, tile), jnp.float32),
+            jax.ShapeDtypeStruct((1, tile), jnp.float32),
+        ),
+        in_specs=[pl.BlockSpec(memory_space=pltpu.SMEM), vmem, vmem, vmem, vmem],
+        out_specs=(vmem, vmem),
+        scratch_shapes=[
+            pltpu.VMEM((n_block, HALF, LANES), jnp.float32),
+            pltpu.VMEM((n_block, HALF, LANES), jnp.float32),
+            pltpu.VMEM((cells, cells), jnp.bfloat16),
+            pltpu.VMEM((cells, cells), jnp.bfloat16),
+            pltpu.VMEM((CLASSES, cells), jnp.float32),
+            pltpu.VMEM((CLASSES, cells), jnp.float32),
+            pltpu.VMEM((cells // LANES, CLASSES, LANES), jnp.float32),
+            pltpu.VMEM((cells // LANES, 8, LANES), jnp.float32),
+            dma((n_block,)),
+            dma((n_block,)),
+            dma((n_block,)),
+            dma((n_block,)),
+            dma((n_block,)),
+            dma,
+        ],
+        compiler_params=pltpu.CompilerParams(collective_id=0, has_side_effects=True),
+    )(counts, coords, final_coords, growth, labels[None, :])
+
+
 def solution(mesh):
     placed = (
         P("pair", None, ("row", "col")),
@@ -124,10 +448,21 @@
         P(),
         P(("row", "col")),
     )
-    return jax.shard_map(
-        per_device,
-        mesh=mesh,
-        in_specs=placed,
-        out_specs=(P("pair", None, ("row", "col")), P("pair", ("row", "col"))),
-        check_vma=False,
-    )
+    out = (P("pair", None, ("row", "col")), P("pair", ("row", "col")))
+
+    def whole(coords, final_coords, growth, counts, labels):
+        cells = coords.shape[2]
+        blocks = mesh.shape["row"] * mesh.shape["col"]
+        fits = (
+            2 * cells == LANES * blocks
+            and blocks % 2 == 0
+            and coords.shape[0] == mesh.shape["pair"]
+            and HALF < coords.shape[1] < 2 * HALF - 1
+            and 4 * cells * cells <= FUSED_BYTES
+        )
+        body = per_device_fused if fits else per_device
+        return jax.shard_map(
+            body, mesh=mesh, in_specs=placed, out_specs=out, check_vma=False
+        )(coords, final_coords, growth, counts, labels)
+
+    return whole

time: 185 us -> 23.7 us (0.13)
  waiting for transfers between devices: 81.2 us -> 0 us
  blocking collectives: 62.1 us -> 0 us
  Pallas kernels: 0 us -> 19.6 us
  between operations: 16.5 us -> 0.65 us
  local copies, waits for them, and re-layouts: 9.93 us -> 3.13 us
  starting transfers between devices: 6.55 us -> 0 us
  matrix products: 4.65 us -> 0 us
  other arithmetic: 2.9 us -> 0 us
    while x8 -> x0, waiting for transfers between devices: 74.1 us -> none
    all_gather x6 -> x0, blocking collectives: 37 us -> none  [the longest x4 17.4 us: hand_over(): return lax.all_gather(incoming, 'row', axis=1, tiled=True)]
    psum x3 -> x0, blocking collectives: 25.2 us -> none  [the longest x1 11.8 us: per_device(): start_rows = lax.psum(start_terms, 'col')]
    pallas_call x0 -> x1, Pallas kernels: none -> 19.6 us  [per_device_fused(): pl.pallas_call(functools.partial(fused, (n_pair, n_row, n_col, tile)), ou...]
    ppermute x5 -> x0, waiting for transfers between devices: 7.07 us -> none  [shifted_2(): return lax.ppermute(block, axis, route)]
    ppermute x5 -> x0, starting transfers between devices: 6.45 us -> none  [shifted_2(): return lax.ppermute(block, axis, route)]
    while x4 -> x0, matrix products: 3.85 us -> none
    while x8 -> x0, local copies, waits for them, and re-layouts: 3.59 us -> none
  transfers between devices with their start and end apart: 9 -> 0, of which waited for: 8 -> 0; matrix products, arithmetic and copies ran while one was open for 2% -> 0% of each run, Pallas kernels for 0% -> 0%
where the time goes in v1:
time: 23.7 us; the launch traced here: 23.4 us
  Pallas kernels  19.6 us (83%)
  local copies, waits for them, and re-layouts  3.13 us (13%)
  between operations  0.65 us (3%)
    pallas_call x1, Pallas kernels, per_device_fused(): pl.pallas_call(functools.partial(fused, (n_pair, n_row, n_col, tile)), ou...  19.6 us
    unnamed x5, local copies, waits for them, and re-layouts  3.13 us

profile of v1, /device:TPU:0, one launch (start us, length us, event | category | flops | bytes accessed | tf_op | source)
XLA Modules:
  0.0 23.4 jit_solution(9270499078661640129)
XLA Ops:
  0.6 1.3 %copy.7.coords_ref = f32[1,30,64]{2,1,0:T(8,128)} copy(f32[1,30,64]{2,0,1:T(1,128)} %param.5) | data formatting | bytes 15360 | tf_op args[0]
  1.9 19.6 %shard_map.68 = (f32[1,16,64]{2,1,0:T(8,128)}, f32[1,64]{1,0:T(1,128)}) custom-call(s32[5]{0:T(128)} %counts_ref.1, f32[1,30,64]{2,1,0:T(8,128)} %copy.7.coords_ref, f32[30,64]{1,0:T(8,128)} %final_ref.1, f32[1,64]{1,0:T(1,128)} %growth_ref.1, s32[1,64]{1,0:T(1,128)} %bitcast.1), custom_call_target="tpu_custom_call" | custom-call | tf_op jit(solution)/shard_map/pallas_call | solution.py:415
  21.6 0.0 copy-start
  21.6 1.3 %copy.10 = f32[1,16,64]{2,1,0:T(8,128)} copy(f32[1,16,64]{2,1,0:T(8,128)} %get-tuple-element.4) | data formatting | bytes 8192
  22.9 0.0 copy-done
  22.9 0.5 %copy.11 = f32[1,64]{1,0:T(1,128)} copy(f32[1,64]{1,0:T(1,128)S(1)} %copy-done) | data formatting | bytes 512
Async XLA Ops:
  21.6 1.3 %copy-start = (f32[1,64]{1,0:T(1,128)S(1)}, f32[1,64]{1,0:T(1,128)}, u32[]{:S(2)}) copy-start(f32[1,64]{1,0:T(1,128)} %get-tuple-element.5) | copy-start | bytes 772

commit v2 on v1

--- a/solution.py
+++ b/solution.py
@@ -191,13 +191,14 @@
     x_recv,
     y_send,
     y_recv,
+    z_send,
     f_send,
     f_recv,
 ):
     n_pair, n_row, n_col, tile = sizes
     n_block = n_row * n_col
     cells = n_block * tile
-    pca = coords_ref.shape[1]
+    pca = coords_ref.shape[0]
     last = n_pair - 1
     pair_at = lax.axis_index("pair")
     row_at = lax.axis_index("row")
@@ -218,13 +219,11 @@
 
     @pl.when(not_last)
     def _():
-        for step in range(n_block):
-            _, r, c = peer(step)
-            pl.semaphore_signal(
-                barrier, inc=1, device_id=(pair_at + 1, r, c), device_id_type=MESH
-            )
-
-    xg[mine] = packed(coords_ref[0], growth_ref[...])
+        pl.semaphore_signal(
+            barrier, inc=1, device_id=(pair_at + 1, row_at, col_at), device_id_type=MESH
+        )
+
+    xg[mine] = packed(coords_ref[:, 0, :], growth_ref[...])
 
     @pl.when(is_last)
     def _():
@@ -232,7 +231,7 @@
 
     @pl.when(not_first)
     def _():
-        pl.semaphore_wait(barrier, 2 * n_block - 1)
+        pl.semaphore_wait(barrier, n_block)
 
     @pl.when(pair_at == 0)
     def _():
@@ -249,14 +248,24 @@
             device_id_type=MESH,
         )
 
-    def y_copy(step, source, pair):
+    def final_copy(step):
         other, r, c = peer(step)
         return pltpu.make_async_remote_copy(
-            src_ref=source.at[mine],
+            src_ref=yg.at[mine],
             dst_ref=yg.at[mine],
-            send_sem=y_send.at[step],
+            send_sem=z_send.at[step],
             recv_sem=y_recv.at[mine],
-            device_id=(pair, r, c),
+            device_id=(pair_at, r, c),
+            device_id_type=MESH,
+        )
+
+    def relay(block):
+        return pltpu.make_async_remote_copy(
+            src_ref=xg.at[block],
+            dst_ref=yg.at[block],
+            send_sem=y_send.at[block],
+            recv_sem=y_recv.at[block],
+            device_id=(jnp.maximum(pair_at - 1, 0), row_at, col_at),
             device_id_type=MESH,
         )
 
@@ -273,36 +282,25 @@
     for step in range(1, n_block):
         x_copy(step).start()
 
-    @pl.when(not_first)
-    def _():
-        for step in range(n_block):
-            y_copy(step, xg, pair_at - 1).start()
-
-    z_send = f_send
-
-    @pl.when(is_last)
-    def _():
-        for step in range(1, n_block):
-            other, r, c = peer(step)
-            pltpu.make_async_remote_copy(
-                src_ref=yg.at[mine],
-                dst_ref=yg.at[mine],
-                send_sem=z_send.at[step],
-                recv_sem=y_recv.at[mine],
-                device_id=(pair_at, r, c),
-                device_id_type=MESH,
-            ).start()
-
-    for step in range(1, n_block):
-        other, _, _ = peer(step)
-        arrival(xg, x_recv, other).wait_recv()
-    for step in range(1, n_block):
-        other, _, _ = peer(step)
-        arrival(yg, y_recv, other).wait_recv()
-
-    @pl.when(not_last)
-    def _():
-        arrival(yg, y_recv, mine).wait_recv()
+        @pl.when(is_last)
+        def _(step=step):
+            final_copy(step).start()
+
+    for block in range(n_block):
+
+        @pl.when(mine != block)
+        def _(block=block):
+            arrival(xg, x_recv, block).wait_recv()
+
+        @pl.when(not_first)
+        def _(block=block):
+            relay(block).start()
+
+    for block in range(n_block):
+
+        @pl.when(not_last | (mine != block))
+        def _(block=block):
+            arrival(yg, y_recv, block).wait_recv()
 
     source_number = counts_ref[pair_at]
     target_number = counts_ref[pair_at + 1]
@@ -357,7 +355,7 @@
     f_copy = pltpu.make_async_remote_copy(
         src_ref=fout,
         dst_ref=fin,
-        send_sem=f_send.at[0],
+        send_sem=f_send,
         recv_sem=f_recv,
         device_id=(jnp.maximum(pair_at - 1, 0), row_at, col_at),
         device_id_type=MESH,
@@ -386,21 +384,14 @@
 
     @pl.when(not_first)
     def _():
-        for step in range(n_block):
-            y_copy(step, xg, pair_at - 1).wait_send()
+        for block in range(n_block):
+            relay(block).wait_send()
         f_copy.wait_send()
 
     @pl.when(is_last)
     def _():
         for step in range(1, n_block):
-            pltpu.make_async_remote_copy(
-                src_ref=yg.at[mine],
-                dst_ref=yg.at[mine],
-                send_sem=z_send.at[step],
-                recv_sem=y_recv.at[mine],
-                device_id=(pair_at, row_at, col_at),
-                device_id_type=MESH,
-            ).wait_send()
+            final_copy(step).wait_send()
 
 
 def per_device_fused(coords, final_coords, growth, counts, labels):
@@ -415,8 +406,8 @@
     return pl.pallas_call(
         functools.partial(fused, (n_pair, n_row, n_col, tile)),
         out_shape=(
-            jax.ShapeDtypeStruct((1, CLASSES, tile), jnp.float32),
-            jax.ShapeDtypeStruct((1, tile), jnp.float32),
+            pltpu.VMEM((1, CLASSES, tile), jnp.float32),
+            pltpu.VMEM((1, tile), jnp.float32),
         ),
         in_specs=[pl.BlockSpec(memory_space=pltpu.SMEM), vmem, vmem, vmem, vmem],
         out_specs=(vmem, vmem),
@@ -435,9 +426,10 @@
             dma((n_block,)),
             dma((n_block,)),
             dma,
+            dma,
         ],
         compiler_params=pltpu.CompilerParams(collective_id=0, has_side_effects=True),
-    )(counts, coords, final_coords, growth, labels[None, :])
+    )(counts, jnp.transpose(coords, (1, 0, 2)), final_coords, growth, labels[None, :])
 
 
 def solution(mesh):

time: 23.7 us -> 18.9 us (0.80)
  Pallas kernels: 19.6 us -> 16.9 us
  local copies, waits for them, and re-layouts: 3.13 us -> 1.11 us
    pallas_call x1, Pallas kernels: 19.6 us -> 16.9 us  [per_device_fused(): pl.pallas_call(functools.partial(fused, (n_pair, n_row, n_col, tile)), ou...]
    unnamed x5 -> x2, local copies, waits for them, and re-layouts: 3.13 us -> 1.11 us
where the time goes in v2:
time: 18.9 us; the launch traced here: 18.7 us
  Pallas kernels  16.9 us (89%)
  local copies, waits for them, and re-layouts  1.11 us (6%)
  between operations  0.64 us (3%)
    pallas_call x1, Pallas kernels, per_device_fused(): pl.pallas_call(functools.partial(fused, (n_pair, n_row, n_col, tile)), ou...  16.9 us
    unnamed x2, local copies, waits for them, and re-layouts  1.11 us

profile of v2, /device:TPU:0, one launch (start us, length us, event | category | flops | bytes accessed | tf_op | source)
XLA Modules:
  0.0 18.7 jit_solution(4525667261926399715)
XLA Ops:
  0.6 16.9 %shard_map.68 = (f32[1,16,64]{2,1,0:T(8,128)S(1)}, f32[1,64]{1,0:T(1,128)S(1)}) custom-call(s32[5]{0:T(128)} %counts_ref.1, f32[30,1,64]{2,1,0:T(1,128)} %bitcast.2, f32[30,64]{1,0:T(8,128)} %final_ref.1, f32[1,64]{1,0:T(1,128)} %growth_ref.1, s32[1,64]{1,0:T(1,128)} %bitcast.3), custom_call_target="tpu_custom_call" | custom-call | tf_op jit(solution)/shard_map/pallas_call | solution.py:406
  17.6 0.6 %copy.9 = f32[1,16,64]{2,1,0:T(8,128)} copy(f32[1,16,64]{2,1,0:T(8,128)S(1)} %get-tuple-element.2) | data formatting | bytes 8192
  18.2 0.5 %copy.10 = f32[1,64]{1,0:T(1,128)} copy(f32[1,64]{1,0:T(1,128)S(1)} %get-tuple-element.3) | data formatting | bytes 512

commit v3 on v2

--- a/solution.py
+++ b/solution.py
@@ -173,12 +173,17 @@
 def fused(
     sizes,
     counts_ref,
+    coords_in,
+    final_in,
+    growth_in,
+    labels_in,
+    fates_ref,
+    mass_ref,
     coords_ref,
     final_ref,
     growth_ref,
     labels_ref,
-    fates_ref,
-    mass_ref,
+    in_sems,
     xg,
     yg,
     k1,
@@ -208,13 +213,15 @@
     not_last = pair_at < last
     not_first = pair_at > 0
 
-    def peer(step):
-        other = lax.rem(mine + step, n_block)
-        return other, other // n_col, lax.rem(other, n_col)
+    def others(act):
+        for block in range(n_block):
+            pl.when(mine != block)(functools.partial(act, block))
 
     barrier = pltpu.get_barrier_semaphore()
-    for step in range(1, n_block):
-        _, r, c = peer(step)
+
+    @others
+    def _(block):
+        r, c = divmod(block, n_col)
         pl.semaphore_signal(barrier, inc=1, device_id=(pair_at, r, c), device_id_type=MESH)
 
     @pl.when(not_last)
@@ -223,6 +230,18 @@
             barrier, inc=1, device_id=(pair_at + 1, row_at, col_at), device_id_type=MESH
         )
 
+    source_loads = (
+        pltpu.make_async_copy(coords_in, coords_ref, in_sems.at[0]),
+        pltpu.make_async_copy(growth_in, growth_ref, in_sems.at[1]),
+    )
+    target_loads = (
+        pltpu.make_async_copy(final_in, final_ref, in_sems.at[2]),
+        pltpu.make_async_copy(labels_in, labels_ref, in_sems.at[3]),
+    )
+    for load in source_loads + target_loads:
+        load.start()
+    for load in source_loads + target_loads:
+        load.wait()
     xg[mine] = packed(coords_ref[:, 0, :], growth_ref[...])
 
     @pl.when(is_last)
@@ -237,23 +256,23 @@
     def _():
         pl.semaphore_wait(barrier, n_block - 1)
 
-    def x_copy(step):
-        other, r, c = peer(step)
+    def x_copy(block):
+        r, c = divmod(block, n_col)
         return pltpu.make_async_remote_copy(
             src_ref=xg.at[mine],
             dst_ref=xg.at[mine],
-            send_sem=x_send.at[step],
+            send_sem=x_send.at[block],
             recv_sem=x_recv.at[mine],
             device_id=(pair_at, r, c),
             device_id_type=MESH,
         )
 
-    def final_copy(step):
-        other, r, c = peer(step)
+    def final_copy(block):
+        r, c = divmod(block, n_col)
         return pltpu.make_async_remote_copy(
             src_ref=yg.at[mine],
             dst_ref=yg.at[mine],
-            send_sem=z_send.at[step],
+            send_sem=z_send.at[block],
             recv_sem=y_recv.at[mine],
             device_id=(pair_at, r, c),
             device_id_type=MESH,
@@ -279,12 +298,13 @@
             device_id_type=MESH,
         )
 
-    for step in range(1, n_block):
-        x_copy(step).start()
+    @others
+    def _(block):
+        x_copy(block).start()
 
         @pl.when(is_last)
-        def _(step=step):
-            final_copy(step).start()
+        def _():
+            final_copy(block).start()
 
     for block in range(n_block):
 
@@ -379,8 +399,9 @@
 
     fates_ref[0] = own_part(pick_f, fates, mine, tile)
 
-    for step in range(1, n_block):
-        x_copy(step).wait_send()
+    @others
+    def _(block):
+        x_copy(block).wait_send()
 
     @pl.when(not_first)
     def _():
@@ -390,8 +411,9 @@
 
     @pl.when(is_last)
     def _():
-        for step in range(1, n_block):
-            final_copy(step).wait_send()
+        @others
+        def _(block):
+            final_copy(block).wait_send()
 
 
 def per_device_fused(coords, final_coords, growth, counts, labels):
@@ -409,9 +431,14 @@
             pltpu.VMEM((1, CLASSES, tile), jnp.float32),
             pltpu.VMEM((1, tile), jnp.float32),
         ),
-        in_specs=[pl.BlockSpec(memory_space=pltpu.SMEM), vmem, vmem, vmem, vmem],
+        in_specs=[pl.BlockSpec(memory_space=pltpu.SMEM)] + [pl.BlockSpec(memory_space=pl.ANY)] * 4,
         out_specs=(vmem, vmem),
         scratch_shapes=[
+            pltpu.VMEM((coords.shape[1], 1, tile), jnp.float32),
+            pltpu.VMEM((coords.shape[1], tile), jnp.float32),
+            pltpu.VMEM((1, tile), jnp.float32),
+            pltpu.VMEM((1, tile), jnp.int32),
+            dma((4,)),
             pltpu.VMEM((n_block, HALF, LANES), jnp.float32),
             pltpu.VMEM((n_block, HALF, LANES), jnp.float32),
             pltpu.VMEM((cells, cells), jnp.bfloat16),

time: 18.9 us -> 17.7 us (0.937)
  Pallas kernels: 16.9 us -> 15.7 us
    pallas_call x1, Pallas kernels: 16.9 us -> 15.7 us  [per_device_fused(): pl.pallas_call(functools.partial(fused, (n_pair, n_row, n_col, tile)), ou...]
where the time goes in v3:
time: 17.7 us; the launch traced here: 17.5 us
  Pallas kernels  15.7 us (89%)
  local copies, waits for them, and re-layouts  1.11 us (6%)
  between operations  0.64 us (4%)
    pallas_call x1, Pallas kernels, per_device_fused(): pl.pallas_call(functools.partial(fused, (n_pair, n_row, n_col, tile)), ou...  15.7 us
    unnamed x2, local copies, waits for them, and re-layouts  1.11 us

profile of v3, /device:TPU:0, one launch (start us, length us, event | category | flops | bytes accessed | tf_op | source)
XLA Modules:
  0.0 17.5 jit_solution(8767900886131284702)
XLA Ops:
  0.6 15.7 %shard_map.68 = (f32[1,16,64]{2,1,0:T(8,128)S(1)}, f32[1,64]{1,0:T(1,128)S(1)}) custom-call(s32[5]{0:T(128)} %counts_ref.1, f32[30,1,64]{2,1,0:T(1,128)} %bitcast.2, f32[30,64]{1,0:T(8,128)} %final_in.1, f32[1,64]{1,0:T(1,128)} %growth_in.1, s32[1,64]{1,0:T(1,128)} %bitcast.3), custom_call_target="tpu_custom_call" | custom-call | tf_op jit(solution)/shard_map/pallas_call | solution.py:428
  16.4 0.6 %copy.9 = f32[1,16,64]{2,1,0:T(8,128)} copy(f32[1,16,64]{2,1,0:T(8,128)S(1)} %get-tuple-element.2) | data formatting | bytes 8192
  17.0 0.5 %copy.10 = f32[1,64]{1,0:T(1,128)} copy(f32[1,64]{1,0:T(1,128)S(1)} %get-tuple-element.3) | data formatting | bytes 512

commit v4 on v3

--- a/solution.py
+++ b/solution.py
@@ -177,8 +177,7 @@
     final_in,
     growth_in,
     labels_in,
-    fates_ref,
-    mass_ref,
+    out_ref,
     coords_ref,
     final_ref,
     growth_ref,
@@ -363,13 +362,16 @@
     scale_v = jnp.where(target_valid, jnp.exp(target_power * jnp.log(ratio)), 0.0)
 
     def transported(weights):
+        rows = weights.shape[0]
         w1, w2 = split2(weights)
         both = dot(jnp.concatenate([w1, w2], axis=0), k1[...], ((1,), (0,)))
-        return both[:CLASSES] + both[CLASSES:] + dot(w1, k2[...], ((1,), (0,)))
-
-    row_totals = transported(jnp.broadcast_to(scale_v, (CLASSES, cells)))[:1]
-    mass = jnp.where(source_valid, source_total * scale_u * row_totals, 0.0)
-    mass_ref[...] = own_part(pick_m, jnp.broadcast_to(mass, (8, cells)), mine, tile)[:1]
+        return both[:rows] + both[rows:] + dot(w1, k2[...], ((1,), (0,)))
+
+    class_values = lax.broadcasted_iota(jnp.int32, (CLASSES, cells), 0).astype(jnp.float32)
+    table = jnp.where((labels == class_values) & target_valid, 1.0, 0.0)
+    spread_v = jnp.broadcast_to(scale_v, (CLASSES, cells))
+    sums = transported(jnp.concatenate([table * scale_v, spread_v], axis=0))
+    row_totals = sums[CLASSES : CLASSES + 1]
     share = jnp.where(source_valid, 1.0 / row_totals, 0.0)
 
     f_copy = pltpu.make_async_remote_copy(
@@ -381,23 +383,25 @@
         device_id_type=MESH,
     )
 
-    @pl.when(is_last)
-    def _():
-        class_values = lax.broadcasted_iota(jnp.int32, (CLASSES, cells), 0).astype(jnp.float32)
-        fin[...] = jnp.where((labels == class_values) & target_valid, 1.0, 0.0)
+    fout[...] = sums[:CLASSES] * share
+
+    @pl.when(is_last & not_first)
+    def _():
+        f_copy.start()
+
+    mass = jnp.where(source_valid, source_total * scale_u * row_totals, 0.0)
+    out_ref[CLASSES:] = own_part(pick_m, jnp.broadcast_to(mass, (8, cells)), mine, tile)
 
     @pl.when(not_last)
     def _():
         f_copy.wait_recv()
-
-    fates = transported(fin[...] * scale_v) * share
-    fout[...] = fates
-
-    @pl.when(not_first)
+        fout[...] = transported(fin[...] * scale_v) * share
+
+    @pl.when(not_last & not_first)
     def _():
         f_copy.start()
 
-    fates_ref[0] = own_part(pick_f, fates, mine, tile)
+    out_ref[:CLASSES] = own_part(pick_f, fout[...], mine, tile)
 
     @others
     def _(block):
@@ -425,14 +429,11 @@
     cells = n_block * tile
     vmem = pl.BlockSpec(memory_space=pltpu.VMEM)
     dma = pltpu.SemaphoreType.DMA
-    return pl.pallas_call(
+    result = pl.pallas_call(
         functools.partial(fused, (n_pair, n_row, n_col, tile)),
-        out_shape=(
-            pltpu.VMEM((1, CLASSES, tile), jnp.float32),
-            pltpu.VMEM((1, tile), jnp.float32),
-        ),
+        out_shape=pltpu.VMEM((CLASSES + 8, tile), jnp.float32),
         in_specs=[pl.BlockSpec(memory_space=pltpu.SMEM)] + [pl.BlockSpec(memory_space=pl.ANY)] * 4,
-        out_specs=(vmem, vmem),
+        out_specs=vmem,
         scratch_shapes=[
             pltpu.VMEM((coords.shape[1], 1, tile), jnp.float32),
             pltpu.VMEM((coords.shape[1], tile), jnp.float32),
@@ -457,6 +458,7 @@
         ],
         compiler_params=pltpu.CompilerParams(collective_id=0, has_side_effects=True),
     )(counts, jnp.transpose(coords, (1, 0, 2)), final_coords, growth, labels[None, :])
+    return result[None, :CLASSES], result[CLASSES : CLASSES + 1]
 
 
 def solution(mesh):

time: 17.7 us -> 17.8 us (level)
    unnamed x2 -> x0, local copies, waits for them, and re-layouts: 1.11 us -> none
    broadcast_in_dim x0 -> x1, local copies, waits for them, and re-layouts: none -> 0.6 us  [per_device_fused(): return (result[None, :CLASSES], result[CLASSES:CLASSES + 1])]
    slice x0 -> x1, local copies, waits for them, and re-layouts: none -> 0.51 us  [per_device_fused(): return (result[None, :CLASSES], result[CLASSES:CLASSES + 1])]
where the time goes in v4:
time: 17.8 us; the launch traced here: 17.5 us
  Pallas kernels  15.8 us (89%)
  local copies, waits for them, and re-layouts  1.11 us (6%)
  between operations  0.64 us (4%)
    pallas_call x1, Pallas kernels, per_device_fused(): pl.pallas_call(functools.partial(fused, (n_pair, n_row, n_col, tile)), ou...  15.8 us
    broadcast_in_dim x1, local copies, waits for them, and re-layouts, per_device_fused(): return (result[None, :CLASSES], result[CLASSES:CLASSES + 1])  0.6 us
    slice x1, local copies, waits for them, and re-layouts, per_device_fused(): return (result[None, :CLASSES], result[CLASSES:CLASSES + 1])  0.51 us

profile of v4, /device:TPU:0, one launch (start us, length us, event | category | flops | bytes accessed | tf_op | source)
XLA Modules:
  0.0 17.5 jit_solution(5522956542725053944)
XLA Ops:
  0.6 15.8 %shard_map.68 = f32[24,64]{1,0:T(8,128)S(1)} custom-call(s32[5]{0:T(128)} %counts_ref.1, f32[30,1,64]{2,1,0:T(1,128)} %bitcast.4, f32[30,64]{1,0:T(8,128)} %final_in.1, f32[1,64]{1,0:T(1,128)} %growth_in.1, s32[1,64]{1,0:T(1,128)} %bitcast.5), custom_call_target="tpu_custom_call" | custom-call | tf_op jit(solution)/shard_map/pallas_call | solution.py:432
  16.4 0.5 %slice.7 = f32[1,64]{1,0:T(1,128)} slice(f32[24,64]{1,0:T(8,128)S(1)} %shard_map.68), slice={[16:17], [0:64]} | slice | bytes 512 | tf_op jit(solution)/shard_map/slice | solution.py:461
  16.9 0.6 %slice_bitcast_fusion = f32[1,16,64]{2,1,0:T(8,128)} fusion(f32[24,64]{1,0:T(8,128)S(1)} %shard_map.68), kind=kLoop, calls=%fused_computation | loop fusion | bytes 8192 | tf_op jit(solution)/shard_map/broadcast_in_dim | solution.py:461

commit v5 on v3

--- a/solution.py
+++ b/solution.py
@@ -123,6 +123,7 @@
 LANES = 128
 HALF = 16
 BIG = 1e30
+LIFT = 2.0**57
 MESH = pl.DeviceIdType.MESH
 
 
@@ -350,7 +351,7 @@
         rows = slice(j * LANES, (j + 1) * LANES)
         values = jnp.exp(dot(left[:, rows], right, ((0,), (0,))))
         totals = totals + jnp.sum(values, axis=0, keepdims=True)
-        high, low = split2(values)
+        high, low = split2(values * LIFT)
         k1[rows, :] = high
         k2[rows, :] = low
     scale_u = jnp.where(source_valid, jnp.sqrt(growth / source_total / totals), 0.0)
@@ -358,14 +359,14 @@
     u12 = jnp.concatenate([u1, u2], axis=0)
     column = dot(u12, k1[...], ((1,), (1,)))
     column_low = dot(u1, k2[...], ((1,), (1,)))
-    column = column[:1] + column[HALF : HALF + 1] + column_low[:1]
+    column = (column[:1] + column[HALF : HALF + 1] + column_low[:1]) * (1.0 / LIFT)
     ratio = 1.0 / target_total / jnp.where(target_valid, column, 1.0)
     scale_v = jnp.where(target_valid, jnp.exp(target_power * jnp.log(ratio)), 0.0)
 
     def transported(weights):
         w1, w2 = split2(weights)
         both = dot(jnp.concatenate([w1, w2], axis=0), k1[...], ((1,), (0,)))
-        return both[:CLASSES] + both[CLASSES:] + dot(w1, k2[...], ((1,), (0,)))
+        return (both[:CLASSES] + both[CLASSES:] + dot(w1, k2[...], ((1,), (0,)))) * (1.0 / LIFT)
 
     row_totals = transported(jnp.broadcast_to(scale_v, (CLASSES, cells)))[:1]
     mass = jnp.where(source_valid, source_total * scale_u * row_totals, 0.0)

time: 17.7 us -> 17.9 us (1.011)
  Pallas kernels: 15.7 us -> 15.9 us
where the time goes in v5:
time: 17.9 us; the launch traced here: 17.6 us
  Pallas kernels  15.9 us (89%)
  local copies, waits for them, and re-layouts  1.11 us (6%)
  between operations  0.64 us (4%)
    pallas_call x1, Pallas kernels, per_device_fused(): pl.pallas_call(functools.partial(fused, (n_pair, n_row, n_col, tile)), ou...  15.9 us
    unnamed x2, local copies, waits for them, and re-layouts  1.11 us

profile of v5, /device:TPU:0, one launch (start us, length us, event | category | flops | bytes accessed | tf_op | source)
XLA Modules:
  0.0 17.6 jit_solution(17409990891763950952)
XLA Ops:
  0.6 15.9 %shard_map.68 = (f32[1,16,64]{2,1,0:T(8,128)S(1)}, f32[1,64]{1,0:T(1,128)S(1)}) custom-call(s32[5]{0:T(128)} %counts_ref.1, f32[30,1,64]{2,1,0:T(1,128)} %bitcast.2, f32[30,64]{1,0:T(8,128)} %final_in.1, f32[1,64]{1,0:T(1,128)} %growth_in.1, s32[1,64]{1,0:T(1,128)} %bitcast.3), custom_call_target="tpu_custom_call" | custom-call | tf_op jit(solution)/shard_map/pallas_call | solution.py:429
  16.5 0.6 %copy.9 = f32[1,16,64]{2,1,0:T(8,128)} copy(f32[1,16,64]{2,1,0:T(8,128)S(1)} %get-tuple-element.2) | data formatting | bytes 8192
  17.1 0.5 %copy.10 = f32[1,64]{1,0:T(1,128)} copy(f32[1,64]{1,0:T(1,128)S(1)} %get-tuple-element.3) | data formatting | bytes 512
